TPU v7x, 32 devices: a whole 2x2x4 slice. The times are simulated.
32 devices in a mesh: cand: 4 (over x, core), seq: 8 (over z, y).
Axes of the slice: x: 2, y: 2, z: 4, core: 2. Of those that a mesh axis runs over, the one named last changes fastest.
Arguments:
- latent: bfloat16 [4, 384, 3072], P('cand', 'seq'), may hold values from -0.59765625 to 0.59765625
- timesteps: int32 [4], replicated, may hold values from 0 to 999
- positions: int32 [3, 384], replicated, may hold values from 0 to 63
- mod_weight: bfloat16 [3072, 9216], P('cand', 'seq'), may hold values from -0.109375 to 0.109375
- input_weight: bfloat16 [3072, 16, 384], P('cand', 'seq'), may hold values from -0.109375 to 0.109375
- output_weight: bfloat16 [16, 128, 3072], P('seq', None, 'cand'), may hold values from -0.75 to 0.75
- cotangent: bfloat16 [4, 384, 3072], P('cand', 'seq'), may hold values from -6 to 6
Outputs:
- block_out: bfloat16 [4, 384, 3072], P('cand', 'seq')
- latent_grad: float32 [4, 384, 3072], P('cand', 'seq')
All inputs are finite; a program needn't handle non-finite values.
Results may differ from a plain program's by a relative error of at most 0.033.
Values may be sent and summed in bfloat16 or wider, within the bound.
A program may use at most 128 MiB of HBM per device.

v0:
```python
import jax
import jax.numpy as jnp
import numpy as np
from jax import lax
from jax.sharding import PartitionSpec as P

HEAD = 128
epsilon = 1e-06


def time_embed(timesteps, feature_width):
    half_size = feature_width // 2
    freq_rate = jnp.exp(-jnp.log(10000.0) * jnp.arange(half_size, dtype=jnp.float32) / half_size)
    angles = timesteps.astype(jnp.float32)[:, None] * freq_rate[None, :]
    return jnp.concatenate([jnp.cos(angles), jnp.sin(angles)], axis=1)


def rope_tables(positions, head_size):
    first_size = head_size // 8
    other_size = (head_size - first_size) // 2
    pieces = []
    swapped = []
    sign_vec = []
    offset = 0
    for axis_id, width_part in enumerate((first_size, other_size, other_size)):
        half_size = width_part // 2
        freq_rate = jnp.exp(
            -jnp.log(256.0) * 2.0 * jnp.arange(half_size, dtype=jnp.float32) / width_part
        )
        angle_part = positions[axis_id].astype(jnp.float32)[:, None] * freq_rate[None, :]
        pieces.append(angle_part)
        pieces.append(angle_part)
        swapped += list(range(offset + half_size, offset + width_part)) + list(
            range(offset, offset + half_size)
        )
        sign_vec += [-1.0] * half_size + [1.0] * half_size
        offset += width_part
    angles = jnp.concatenate(pieces, axis=1)
    return (
        jnp.cos(angles),
        jnp.sin(angles),
        np.array(swapped, np.int32),
        np.array(sign_vec, np.float32),
    )


def rotate(values, tables):
    cos_tab, sin_tab, swapped, sign_vec = tables
    return values * cos_tab + values[..., swapped] * sign_vec * sin_tab


def unrotate(values, tables):
    cos_tab, sin_tab, swapped, sign_vec = tables
    return values * cos_tab - (values * sin_tab)[..., swapped] * sign_vec


def rms_norm(values):
    inverse = lax.rsqrt(jnp.mean(values * values, -1, keepdims=True) + epsilon)
    return (values * inverse, inverse)


def rms_back(d_normed, normed, inverse):
    return inverse * (d_normed - normed * jnp.mean(d_normed * normed, -1, keepdims=True))


def layer_norm(values):
    centred = values - jnp.mean(values, -1, keepdims=True)
    inverse_std = lax.rsqrt(jnp.mean(centred * centred, -1, keepdims=True) + epsilon)
    return (centred * inverse_std, inverse_std)


def layer_norm_back(d_normed, normed, inverse_std):
    return inverse_std * (
        d_normed
        - jnp.mean(d_normed, -1, keepdims=True)
        - normed * jnp.mean(d_normed * normed, -1, keepdims=True)
    )


def times_transposed(left, right):
    return lax.dot_general(
        left, right, (((1,), (1,)), ((), ())), preferred_element_type=jnp.float32
    )


def attend(projected, tables):
    length, groups, triple = projected.shape
    head_size = triple // 3
    grouped = jnp.transpose(projected.reshape(length, groups, 3, head_size), (2, 1, 0, 3))
    query_n, query_inv = rms_norm(grouped[0])
    key_n, key_inv = rms_norm(grouped[1])
    q_rot = rotate(query_n, tables).astype(jnp.bfloat16)
    k_rot = rotate(key_n, tables).astype(jnp.bfloat16)
    values = grouped[2].astype(jnp.bfloat16)
    score_scale = head_size ** (-0.5)
    scores = (
        jnp.einsum("gld,gmd->glm", q_rot, k_rot, preferred_element_type=jnp.float32) * score_scale
    )
    weights = jnp.exp(scores - head_size**0.5)
    probs = weights / jnp.sum(weights, -1, keepdims=True)
    probs_low = probs.astype(jnp.bfloat16)
    heads_out = jnp.einsum("glm,gmd->gld", probs_low, values, preferred_element_type=jnp.float32)
    attended = (
        jnp.transpose(heads_out, (1, 0, 2)).reshape(length, groups * head_size).astype(jnp.bfloat16)
    )
    saved = (q_rot, k_rot, values, probs, probs_low, query_n, query_inv, key_n, key_inv)
    return (attended, saved)


def attend_back(d_attended, saved, tables):
    q_rot, k_rot, values, probs, probs_low, query_n, query_inv, key_n, key_inv = saved
    groups, length, head_size = q_rot.shape
    score_scale = head_size ** (-0.5)
    d_heads = jnp.transpose(d_attended.reshape(length, groups, head_size), (1, 0, 2))
    d_values = jnp.einsum("glm,gld->gmd", probs_low, d_heads, preferred_element_type=jnp.float32)
    d_probs = jnp.einsum("gld,gmd->glm", d_heads, values, preferred_element_type=jnp.float32)
    d_scores = (probs * (d_probs - jnp.sum(probs * d_probs, -1, keepdims=True))).astype(
        jnp.bfloat16
    )
    d_qrot = (
        jnp.einsum("glm,gmd->gld", d_scores, k_rot, preferred_element_type=jnp.float32)
        * score_scale
    )
    d_krot = (
        jnp.einsum("glm,gld->gmd", d_scores, q_rot, preferred_element_type=jnp.float32)
        * score_scale
    )
    d_query = rms_back(unrotate(d_qrot, tables), query_n, query_inv)
    d_key = rms_back(unrotate(d_krot, tables), key_n, key_inv)
    stacked = jnp.stack([d_query, d_key, d_values], 0)
    return (
        jnp.transpose(stacked, (2, 1, 0, 3))
        .reshape(length, groups * 3 * head_size)
        .astype(jnp.bfloat16)
    )


def on_device(latent, timesteps, positions, mod_weight, input_weight, output_weight, cotangent):
    width = latent.shape[2]
    groups = input_weight.shape[1]
    group_cols = groups * input_weight.shape[2]
    time_act = jax.nn.silu(time_embed(timesteps, width)).astype(jnp.bfloat16)
    slab_rows = mod_weight.shape[0]
    act_rows = lax.dynamic_slice_in_dim(time_act, lax.axis_index("cand") * slab_rows, slab_rows, 1)
    mod_mine = lax.psum_scatter(
        jnp.dot(act_rows, mod_weight, preferred_element_type=jnp.float32).astype(jnp.bfloat16),
        "cand",
        scatter_dimension=0,
        tiled=True,
    ).astype(jnp.float32)
    modulation = lax.all_gather(mod_mine, "seq", axis=1, tiled=True)[0]
    shift_vec = modulation[:width]
    scale_vec = modulation[width : 2 * width]
    gate_vec = modulation[2 * width :]
    latent_all = lax.all_gather(latent[0], "seq", axis=0, tiled=True)
    length = latent_all.shape[0]
    normed_all, _ = layer_norm(latent_all.astype(jnp.float32))
    modulated = (normed_all * (1.0 + scale_vec) + shift_vec).astype(jnp.bfloat16)
    tables = rope_tables(positions, HEAD)
    piece = lax.all_gather(input_weight, "cand", axis=0, tiled=True).reshape(width, group_cols)
    cot_all = lax.all_gather(cotangent[0], "seq", axis=0, tiled=True)
    w_heads = lax.all_gather(output_weight, "cand", axis=2, tiled=True)
    w_heads = w_heads.reshape(w_heads.shape[0] * w_heads.shape[1], width)
    projected = jnp.dot(modulated, piece, preferred_element_type=jnp.float32)
    attended, saved = attend(projected.reshape(length, groups, 3 * HEAD), tables)
    mixed_part = jnp.dot(attended, w_heads, preferred_element_type=jnp.float32).astype(jnp.bfloat16)
    mixed = lax.psum_scatter(mixed_part, "seq", scatter_dimension=0, tiled=True).astype(jnp.float32)
    latent_rows = latent[0].astype(jnp.float32)
    block_out = (latent_rows + gate_vec * mixed).astype(jnp.bfloat16)
    d_mixed = (cot_all.astype(jnp.float32) * gate_vec).astype(jnp.bfloat16)
    d_attended = times_transposed(d_mixed, w_heads).astype(jnp.bfloat16)
    d_projected = attend_back(d_attended, saved, tables)
    d_modulated = lax.psum_scatter(
        times_transposed(d_projected, piece).astype(jnp.bfloat16),
        "seq",
        scatter_dimension=0,
        tiled=True,
    ).astype(jnp.float32)
    normed, inverse_std = layer_norm(latent_rows)
    latent_grad = cotangent[0].astype(jnp.float32) + layer_norm_back(
        d_modulated * (1.0 + scale_vec), normed, inverse_std
    )
    return (block_out[None], latent_grad[None])


def solution(mesh):
    placed = (
        P("cand", "seq", None),
        P(),
        P(),
        P("cand", "seq"),
        P("cand", "seq", None),
        P("seq", None, "cand"),
        P("cand", "seq", None),
    )
    return jax.shard_map(
        on_device,
        mesh=mesh,
        in_specs=placed,
        out_specs=(P("cand", "seq", None), P("cand", "seq", None)),
        check_vma=False,
    )
```

profile of v0, /device:TPU:0, one launch (start us, length us, event | category | flops | bytes accessed | tf_op | source)
XLA Modules:
  0.0 379.9 jit_solution(7271335132875156814)
XLA Ops:
  11.9 8.7 %all-reduce = bf16[4,1152]{1,0:T(4,128)(2,1)S(1)} all-reduce(bf16[4,1152]{1,0:T(4,128)(2,1)S(1)} %convolution_convert_fusion.1), channel_id=4, replica_groups=mesh['cand'=4,'seq'=8] {'cand'}, use_global_device_ids=true, to_apply=%region_0.1.clone | all-reduce | flops 4608 | bytes 18432
  21.2 31.6 %all_gather.15 = f32[1,9216]{1,0:T(1,128)S(1)} all-gather(f32[1,1152]{1,0:T(1,128)S(1)} %dynamic-slice_convert_fusion), channel_id=1, replica_groups=mesh['cand'=4,'seq'=8] {'seq'}, dimensions={1}, use_global_device_ids=true | all-gather | bytes 41472 | tf_op jit(solution)/shard_map/all_gather | solution.py:151
  54.9 10.1 %all-gather.11.cloned.1.call-done = bf16[1,384,3072]{2,1,0:T(8,128)(2,1)} async-done(((bf16[1,48,3072]{2,1,0:T(8,128)(2,1)}), bf16[1,384,3072]{2,1,0:T(8,128)(2,1)}) %all-gather.11.cloned.1.call-update) | async-done | bytes 2359312 | tf_op jit(solution)/shard_map/all_gather | solution.py:155
  65.0 2.2 convert_reduce_fusion
  68.1 16.7 %all-gather.9.cloned.1.call-done = bf16[2,128,3072]{2,1,0:T(8,128)(2,1)} async-done(((bf16[2,128,768]{2,1,0:T(8,128)(2,1)}), bf16[2,128,3072]{2,1,0:T(8,128)(2,1)}) %all-gather.9.cloned.1.call-update) | async-done | bytes 1572880 | tf_op jit(solution)/shard_map/all_gather | solution.py:162
  84.8 54.0 %all-gather.13.cloned.1.call-done = bf16[1,384,3072]{2,1,0:T(8,128)(2,1)} async-done(((bf16[1,48,3072]{2,1,0:T(8,128)(2,1)}), bf16[1,384,3072]{2,1,0:T(8,128)(2,1)}) %all-gather.13.cloned.1.call-update) | async-done | bytes 2359312 | tf_op jit(solution)/shard_map/all_gather | solution.py:161
  138.9 3.1 fusion.24
  142.0 34.3 %all-gather.7.cloned.1.call-done = bf16[3072,2,384]{2,1,0:T(2,128)(2,1)} async-done(((bf16[768,2,384]{2,1,0:T(2,128)(2,1)}), bf16[3072,2,384]{2,1,0:T(2,128)(2,1)}) %all-gather.7.cloned.1.call-update) | async-done | bytes 4718608 | tf_op jit(solution)/shard_map/all_gather | solution.py:160
  176.3 5.3 %copy.73 = bf16[384,8,2,384]{3,1,2,0:T(8,128)(2,1)} copy(bf16[384,8,2,384]{3,2,1,0:T(2,128)(2,1)} %bitcast.164) | data formatting | bytes 9437184
  181.5 6.7 %copy.42 = bf16[3072,768]{0,1:T(8,128)(2,1)} copy(bf16[3072,768]{1,0:T(8,128)(2,1)} %bitcast.160) | data formatting | bytes 9437184 | tf_op jit(solution)/shard_map/reshape | solution.py:160
  188.3 5.5 %fusion.19 = f32[3,2,384,128]{2,3,0,1:T(8,128)S(1)} fusion(bf16[2,3,128,3072]{3,2,1,0:T(8,128)(2,1)} %bitcast.165, bf16[1,384,3072]{2,1,0:T(8,128)(2,1)} %all-gather.11.cloned.1.call-done, f32[3072]{0:T(1024)S(1)} %bitcast.175, f32[3072]{0:T(1024)S(1)} %bitcast.170, f32[384]{0:T(512)S(1)} %add_rsqrt_fusion.2, f32[384]{0:T(512)S(1)} %broadcast_multiply_fusion.9), kind=kOutput, calls=%fused_computation.27 | convolution fusion | flops 1819017216 | bytes 8285184 | tf_op jit(solution)/shard_map/dot_general | solution.py:164
  197.0 2.2 gather_fusion
  199.2 2.9 gather_fusion.1
  202.1 2.5 fusion.58
  206.1 2.1 multiply_reduce_fusion
  213.7 2.9 gather_fusion.3
  216.6 2.1 copy.55
  218.7 2.9 gather_fusion.2
  221.6 2.0 multiply_reduce_fusion.2
  225.3 3.5 convolution_convert_fusion
  228.9 4.0 %bitcast_convert_fusion = bf16[384,3072]{1,0:T(8,128)(2,1)} fusion(bf16[2,128,3072]{2,1,0:T(8,128)(2,1)} %all-gather.9.cloned.1.call-done, f32[2,384,384]{1,2,0:T(8,128)S(1)} %get-tuple-element.31, f32[3,2,384,128]{2,3,0,1:T(8,128)} %copy-done.10), kind=kOutput, calls=%fused_computation.15 | convolution fusion | flops 681050112 | bytes 5308416 | tf_op jit(solution)/shard_map/dot_general | solution.py:166
  234.3 64.3 %reduce-scatter.5.cloned.1.call-done = bf16[48,3072]{1,0:T(8,128)(2,1)} async-done(((bf16[384,3072]{1,0:T(8,128)(2,1)}), bf16[48,3072]{1,0:T(8,128)(2,1)}) %reduce-scatter.5.cloned.1.call-update) | async-done | bytes 294928 | tf_op jit(solution)/shard_map/reduce_scatter | solution.py:173
  299.8 70.9 %reduce-scatter.3.cloned.1.call-done = bf16[48,3072]{1,0:T(8,128)(2,1)} async-done(((bf16[384,3072]{1,0:T(8,128)(2,1)}), bf16[48,3072]{1,0:T(8,128)(2,1)}) %reduce-scatter.3.cloned.1.call-update) | async-done | bytes 294928 | tf_op jit(solution)/shard_map/reduce_scatter | solution.py:167
  370.8 2.3 fusion.39
  (121 shorter events, 22.7 us)
Async XLA Ops:
  7.2 4.3 %copy-start = (bf16[768,1152]{1,0:T(8,128)(2,1)S(1)}, bf16[768,1152]{1,0:T(8,128)(2,1)}, u32[]{:S(2)}) copy-start(bf16[768,1152]{1,0:T(8,128)(2,1)} %param.16) | copy-start | bytes 5308420
  7.2 2.9 copy-start.30
  7.2 2.9 copy-start.29
  7.2 3.5 copy-start.27
  7.2 57.8 %all-gather.11.cloned.1.call-start = ((), (), s32[]{:S(2)}) async-start(), calls=%async_computation.6 | async-start | bytes 2654208 | tf_op jit(solution)/shard_map/all_gather | solution.py:155
  7.9 76.9 %all-gather.9.cloned.1.call-start = ((), (), s32[]{:S(2)}) async-start(), calls=%async_computation.3 | async-start | bytes 1966080 | tf_op jit(solution)/shard_map/all_gather | solution.py:162
  8.7 130.2 %all-gather.13.cloned.1.call-start = ((), (), s32[]{:S(2)}) async-start(), calls=%async_computation.7 | async-start | bytes 2654208 | tf_op jit(solution)/shard_map/all_gather | solution.py:161
  9.4 43.4 %copy-start.28 = (s32[128]{0:T(128)S(1)}, s32[128]{0:T(128)}, u32[]{:S(2)}) copy-start(s32[128]{0:T(128)} %constant.73) | copy-start | bytes 1540
  9.4 166.8 %all-gather.7.cloned.1.call-start = ((), (), s32[]{:S(2)}) async-start(), calls=%async_computation.2 | async-start | bytes 5898240 | tf_op jit(solution)/shard_map/all_gather | solution.py:160
  10.0 288.6 %reduce-scatter.5.cloned.1.call-start = ((), (), s32[]{:S(2)}) async-start(), calls=%async_computation.5 | async-start | bytes 2654208 | tf_op jit(solution)/shard_map/reduce_scatter | solution.py:173
  54.9 84.0 %copy-start.22 = (f32[1,3072]{1,0:T(1,128)}, f32[1,3072]{1,0:T(1,128)S(1)}, u32[]{:S(2)}) copy-start(f32[1,3072]{1,0:T(1,128)S(1)} %get-tuple-element.23) | copy-start | bytes 36868
  142.0 60.1 %copy-start.18 = (bf16[384,256]{0,1:T(8,128)(2,1)}, bf16[384,256]{0,1:T(8,128)(2,1)S(1)}, u32[]{:S(2)}) copy-start(bf16[384,256]{0,1:T(8,128)(2,1)S(1)} %fusion.24) | copy-start | bytes 589828
  194.9 11.2 %copy-start.3 = (f32[2,384,128]{1,2,0:T(8,128)}, f32[2,384,128]{1,2,0:T(8,128)S(1)}, u32[]{:S(2)}) copy-start(f32[2,384,128]{1,2,0:T(8,128)S(1)} %get-tuple-element.12) | copy-start | bytes 1179652
  194.9 13.3 %copy-start.1 = (f32[2,384,128]{1,2,0:T(8,128)}, f32[2,384,128]{1,2,0:T(8,128)S(1)}, u32[]{:S(2)}) copy-start(f32[2,384,128]{1,2,0:T(8,128)S(1)} %get-tuple-element.11) | copy-start | bytes 1179652
  202.1 2.5 copy-start.15
  212.6 9.0 %copy-start.26 = (f32[128]{0:T(128)S(1)}, f32[128]{0:T(128)}, u32[]{:S(2)}) copy-start(f32[128]{0:T(128)} %constant.67.clone) | copy-start | bytes 1540
  212.6 11.8 %slice-start = ((s8[4718592]{0:T(1024)(128)(4,1)}), s8[524288]{0:T(1024)(128)(4,1)S(1)}, s32[]{:S(2)}) async-start(s8[4718592]{0:T(1024)(128)(4,1)} %bitcast.161), calls=%async_computation.8 | async-start | bytes 1048576
  218.6 5.0 %copy-start.25 = (f32[2,384]{1,0:T(2,128)S(1)}, f32[2,384]{1,0:T(2,128)}, u32[]{:S(2)}) copy-start(f32[2,384]{1,0:T(2,128)} %copy-done.24) | copy-start | bytes 9220
  221.5 2.4 copy-start.14
  221.6 2.7 copy-start.17
  221.6 3.8 slice-start.1
  228.9 141.9 %reduce-scatter.3.cloned.1.call-start = ((), (), s32[]{:S(2)}) async-start(), calls=%async_computation.4 | async-start | bytes 2654208 | tf_op jit(solution)/shard_map/reduce_scatter | solution.py:167
  232.9 137.8 %copy-start.16 = (bf16[1,48,3072]{2,1,0:T(8,128)(2,1)S(1)}, bf16[1,48,3072]{2,1,0:T(8,128)(2,1)}, u32[]{:S(2)}) copy-start(bf16[1,48,3072]{2,1,0:T(8,128)(2,1)} %param.19) | copy-start | bytes 884740
  232.9 137.8 %copy-start.23 = (f32[1,3072]{1,0:T(1,128)S(1)}, f32[1,3072]{1,0:T(1,128)}, u32[]{:S(2)}) copy-start(f32[1,3072]{1,0:T(1,128)} %copy-done.22) | copy-start | bytes 36868
  (15 other events, 26.3 us)
Sparse Core Ops, SparseCore 0:
  10.2 54.7 all-gather.10
  66.5 18.2 all-gather.8
  87.0 51.8 all-gather.12
  140.3 35.9 all-gather.6
  229.0 69.5 reduce-scatter.4
  301.9 68.7 reduce-scatter.2
where the time goes:
time: 381 us; the launch traced here: 380 us
  waiting for transfers between devices  253 us (66%)
  blocking collectives  40.3 us (11%)
  local copies, waits for them, and re-layouts  33.8 us (9%)
  matrix products  24.5 us (6%)
  between operations  14.6 us (4%)
  other arithmetic  13.7 us (4%)
    reduce_scatter x1, waiting for transfers between devices, on_device(): lax.psum_scatter(mixed_part, 'seq', scatter_dimension=0, tiled=True)  70.9 us
    reduce_scatter x1, waiting for transfers between devices, on_device(): lax.psum_scatter(times_transposed(d_projected, piece).astype(jnp.bfloat16...  64.3 us
    all_gather x1, waiting for transfers between devices, on_device(): cot_all = lax.all_gather(cotangent[0], 'seq', axis=0, tiled=True)  54 us
    all_gather x1, waiting for transfers between devices, on_device(): lax.all_gather(input_weight, 'cand', axis=0, tiled=True)  34.3 us
    all_gather x1, blocking collectives, on_device(): modulation = lax.all_gather(mod_mine, 'seq', axis=1, tiled=True)[0]  31.6 us
    all_gather x1, waiting for transfers between devices, on_device(): w_heads = lax.all_gather(output_weight, 'cand', axis=2, tiled=True)  16.7 us
    all_gather x1, waiting for transfers between devices, on_device(): latent_all = lax.all_gather(latent[0], 'seq', axis=0, tiled=True)  10.1 us
    unnamed x68, local copies, waits for them, and re-layouts  9.94 us
  transfers between devices with their start and end apart: 6, of which 6 were waited for; matrix products, arithmetic and copies ran while one was open for 4% of the time, Pallas kernels for 0%

commit v1 on v0

--- a/solution.py
+++ b/solution.py
@@ -6,6 +6,16 @@
 
 HEAD = 128
 epsilon = 1e-06
+
+
+def around_the_ring(value, axis, d):
+    size = lax.axis_size(axis)
+    block, shards = (value, [value])
+    for _ in range(size - 1):
+        block = lax.ppermute(block, axis, [(i, (i + 1) % size) for i in range(size)])
+        shards.insert(0, block)
+    flat = jnp.concatenate(shards, axis=d)
+    return jnp.roll(flat, (lax.axis_index(axis) + 1) * value.shape[d], axis=d)
 
 
 def time_embed(timesteps, feature_width):
@@ -158,7 +168,7 @@
     modulated = (normed_all * (1.0 + scale_vec) + shift_vec).astype(jnp.bfloat16)
     tables = rope_tables(positions, HEAD)
     piece = lax.all_gather(input_weight, "cand", axis=0, tiled=True).reshape(width, group_cols)
-    cot_all = lax.all_gather(cotangent[0], "seq", axis=0, tiled=True)
+    cot_all = around_the_ring(cotangent[0], "seq", 0)
     w_heads = lax.all_gather(output_weight, "cand", axis=2, tiled=True)
     w_heads = w_heads.reshape(w_heads.shape[0] * w_heads.shape[1], width)
     projected = jnp.dot(modulated, piece, preferred_element_type=jnp.float32)

time: 381 us -> 346 us (0.908)
  waiting for transfers between devices: 253 us -> 188 us
  local copies, waits for them, and re-layouts: 33.8 us -> 54.3 us
  other arithmetic: 13.7 us -> 20.8 us
  starting transfers between devices: 0.23 us -> 5.45 us
    all_gather x1 -> x0, waiting for transfers between devices: 54 us -> none  [on_device(): cot_all = lax.all_gather(cotangent[0], 'seq', axis=0, tiled=True)]
    ppermute x0 -> x7, waiting for transfers between devices: none -> 53.7 us  [around_the_ring(): lax.ppermute(block, axis, [(i, (i + 1) % size) for i in range(size)])]
    all_gather x1, waiting for transfers between devices: 34.3 us -> 0.02 us  [on_device(): lax.all_gather(input_weight, 'cand', axis=0, tiled=True)]
    all_gather x1, waiting for transfers between devices: 16.7 us -> 0.01 us  [on_device(): w_heads = lax.all_gather(output_weight, 'cand', axis=2, tiled=True)]
    unnamed x68 -> x55, local copies, waits for them, and re-layouts: 9.94 us -> 24.5 us
    all_gather x1, waiting for transfers between devices: 10.1 us -> 0.02 us  [on_device(): latent_all = lax.all_gather(latent[0], 'seq', axis=0, tiled=True)]
    ppermute x0 -> x7, starting transfers between devices: none -> 5.26 us  [around_the_ring(): lax.ppermute(block, axis, [(i, (i + 1) % size) for i in range(size)])]
    concatenate x1, local copies, waits for them, and re-layouts: 0.32 us -> 5.26 us  [rope_tables(): angles = jnp.concatenate(pieces, axis=1)]
  transfers between devices with their start and end apart: 6 -> 12, of which waited for: 6 -> 8; matrix products, arithmetic and copies ran while one was open for 4% -> 13% of each run, Pallas kernels for 0% -> 0%
where the time goes in v1:
time: 346 us; the launch traced here: 345 us
  waiting for transfers between devices  188 us (54%)
  local copies, waits for them, and re-layouts  54.3 us (16%)
  blocking collectives  37 us (11%)
  matrix products  24.4 us (7%)
  other arithmetic  20.8 us (6%)
  between operations  14.1 us (4%)
  starting transfers between devices  5.45 us (2%)
    reduce_scatter x1, waiting for transfers between devices, on_device(): lax.psum_scatter(mixed_part, 'seq', scatter_dimension=0, tiled=True)  70.9 us
    reduce_scatter x1, waiting for transfers between devices, on_device(): lax.psum_scatter(times_transposed(d_projected, piece).astype(jnp.bfloat16...  62.3 us
    ppermute x7, waiting for transfers between devices, around_the_ring(): lax.ppermute(block, axis, [(i, (i + 1) % size) for i in range(size)])  53.7 us
    all_gather x1, blocking collectives, on_device(): modulation = lax.all_gather(mod_mine, 'seq', axis=1, tiled=True)[0]  31.2 us
    unnamed x55, local copies, waits for them, and re-layouts  24.5 us
  transfers between devices with their start and end apart: 12, of which 8 were waited for; matrix products, arithmetic and copies ran while one was open for 13% of the time, Pallas kernels for 0%

profile of v1, /device:TPU:0, one launch (start us, length us, event | category | flops | bytes accessed | tf_op | source)
XLA Modules:
  0.0 344.5 jit_solution(6128116248542293922)
XLA Ops:
  8.7 3.0 collective-permute-start
  12.5 9.5 %collective-permute-done = bf16[48,3072]{1,0:T(8,128)(2,1)S(1)} collective-permute-done((bf16[48,3072]{1,0:T(8,128)(2,1)}, bf16[48,3072]{1,0:T(8,128)(2,1)S(1)}, u32[]{:S(2)}, u32[]{:S(2)}) %collective-permute-start) | collective-permute-done | bytes 294944 | tf_op jit(solution)/shard_map/ppermute | solution.py:15
  22.3 10.6 %collective-permute-done.1 = bf16[48,3072]{1,0:T(8,128)(2,1)S(1)} collective-permute-done((bf16[48,3072]{1,0:T(8,128)(2,1)S(1)}, bf16[48,3072]{1,0:T(8,128)(2,1)S(1)}, u32[]{:S(2)}, u32[]{:S(2)}) %collective-permute-start.1) | collective-permute-done | bytes 294944 | tf_op jit(solution)/shard_map/ppermute | solution.py:15
  34.5 5.9 %all-reduce = bf16[4,1152]{1,0:T(4,128)(2,1)S(1)} all-reduce(bf16[4,1152]{1,0:T(4,128)(2,1)S(1)} %convolution_convert_fusion.1), channel_id=3, replica_groups=mesh['cand'=4,'seq'=8] {'cand'}, use_global_device_ids=true, to_apply=%region_0.1.clone | all-reduce | flops 4608 | bytes 18432
  41.0 31.2 %all_gather.12 = f32[1,9216]{1,0:T(1,128)S(1)} all-gather(f32[1,1152]{1,0:T(1,128)S(1)} %dynamic-slice_convert_fusion), channel_id=1, replica_groups=mesh['cand'=4,'seq'=8] {'seq'}, dimensions={1}, use_global_device_ids=true | all-gather | bytes 41472 | tf_op jit(solution)/shard_map/all_gather | solution.py:161
  72.2 2.2 collective-permute-start.3
  75.8 10.7 %collective-permute-done.3 = bf16[48,3072]{1,0:T(8,128)(2,1)S(1)} collective-permute-done((bf16[48,3072]{1,0:T(8,128)(2,1)S(1)}, bf16[48,3072]{1,0:T(8,128)(2,1)S(1)}, u32[]{:S(2)}, u32[]{:S(2)}) %collective-permute-start.3) | collective-permute-done | bytes 294944 | tf_op jit(solution)/shard_map/ppermute | solution.py:15
  86.7 11.5 %collective-permute-done.4 = bf16[48,3072]{1,0:T(8,128)(2,1)} collective-permute-done((bf16[48,3072]{1,0:T(8,128)(2,1)S(1)}, bf16[48,3072]{1,0:T(8,128)(2,1)}, u32[]{:S(2)}, u32[]{:S(2)}) %collective-permute-start.4) | collective-permute-done | bytes 294944 | tf_op jit(solution)/shard_map/ppermute | solution.py:15
  98.3 5.3 %concatenate.21 = f32[384,128]{0,1:T(8,128)} concatenate(f32[384,8]{0,1:T(8,128)S(1)} %broadcast_multiply_fusion.6, f32[384,8]{0,1:T(8,128)S(1)} %broadcast_multiply_fusion.6, f32[384,28]{0,1:T(8,128)S(1)} %get-tuple-element.29, f32[384,28]{0,1:T(8,128)S(1)} %get-tuple-element.29, f32[384,28]{0,1:T(8,128)S(1)} %get-tuple-element.28, f32[384,28]{0,1:T(8,128)S(1)} %get-tuple-element.28), dimensions={1} | concatenate | bytes 393216 | tf_op jit(solution)/shard_map/concatenate | solution.py:48
  105.2 3.0 collective-permute-done.5
  109.7 8.3 %collective-permute-done.6 = bf16[48,3072]{1,0:T(8,128)(2,1)} collective-permute-done((bf16[48,3072]{1,0:T(8,128)(2,1)}, bf16[48,3072]{1,0:T(8,128)(2,1)}, u32[]{:S(2)}, u32[]{:S(2)}) %collective-permute-start.6) | collective-permute-done | bytes 294944 | tf_op jit(solution)/shard_map/ppermute | solution.py:15
  136.6 3.1 fusion.22
  141.9 2.4 fusion.3
  144.4 5.3 %copy.73 = bf16[384,8,2,384]{3,1,2,0:T(8,128)(2,1)} copy(bf16[384,8,2,384]{3,2,1,0:T(2,128)(2,1)} %bitcast.157) | data formatting | bytes 9437184
  149.7 6.7 %copy.42 = bf16[3072,768]{0,1:T(8,128)(2,1)} copy(bf16[3072,768]{1,0:T(8,128)(2,1)} %bitcast.153) | data formatting | bytes 9437184 | tf_op jit(solution)/shard_map/reshape | solution.py:170
  156.3 5.5 %fusion.17 = f32[3,2,384,128]{2,3,0,1:T(8,128)S(1)} fusion(bf16[2,3,128,3072]{3,2,1,0:T(8,128)(2,1)} %bitcast.158, bf16[1,384,3072]{2,1,0:T(8,128)(2,1)} %all-gather.9.cloned.1.call-done, f32[3072]{0:T(1024)S(1)} %bitcast.169, f32[3072]{0:T(1024)S(1)} %bitcast.164, f32[384]{0:T(512)S(1)} %add_rsqrt_fusion.2, f32[384]{0:T(512)S(1)} %broadcast_multiply_fusion.9), kind=kOutput, calls=%fused_computation.26 | convolution fusion | flops 1819017216 | bytes 8285184 | tf_op jit(solution)/shard_map/dot_general | solution.py:174
  167.6 2.7 gather_fusion
  181.3 2.7 gather_fusion.2
  186.1 2.7 gather_fusion.3
  193.1 3.5 %convolution_convert_fusion = bf16[384,3072]{1,0:T(8,128)(2,1)} fusion(bf16[384,768]{0,1:T(8,128)(2,1)S(1)} %bitcast.163, bf16[3072,768]{1,0:T(8,128)(2,1)S(1)} %bitcast.156), kind=kOutput, calls=%fused_computation.15 | convolution fusion | flops 1813118976 | bytes 7667712 | tf_op jit(solution)/shard_map/dot_general | solution.py:91
  196.7 4.0 %bitcast_convert_fusion = bf16[384,3072]{1,0:T(8,128)(2,1)} fusion(bf16[2,128,3072]{2,1,0:T(8,128)(2,1)} %all-gather.7.cloned.1.call-done, f32[2,384,384]{1,2,0:T(8,128)S(1)} %get-tuple-element.31, f32[3,2,384,128]{2,3,0,1:T(8,128)} %copy-done.5), kind=kOutput, calls=%fused_computation.13 | convolution fusion | flops 681050112 | bytes 5308416 | tf_op jit(solution)/shard_map/dot_general | solution.py:176
  201.2 62.3 %reduce-scatter.5.cloned.1.call-done = bf16[48,3072]{1,0:T(8,128)(2,1)} async-done(((bf16[384,3072]{1,0:T(8,128)(2,1)}), bf16[48,3072]{1,0:T(8,128)(2,1)}) %reduce-scatter.5.cloned.1.call-update) | async-done | bytes 294928 | tf_op jit(solution)/shard_map/reduce_scatter | solution.py:183
  264.7 70.9 %reduce-scatter.3.cloned.1.call-done = bf16[48,3072]{1,0:T(8,128)(2,1)} async-done(((bf16[384,3072]{1,0:T(8,128)(2,1)}), bf16[48,3072]{1,0:T(8,128)(2,1)}) %reduce-scatter.3.cloned.1.call-update) | async-done | bytes 294928 | tf_op jit(solution)/shard_map/reduce_scatter | solution.py:177
  335.6 2.4 fusion.35
  (120 shorter events, 54.9 us)
Async XLA Ops:
  7.2 25.7 %copy-start = (bf16[768,1152]{1,0:T(8,128)(2,1)S(1)}, bf16[768,1152]{1,0:T(8,128)(2,1)}, u32[]{:S(2)}) copy-start(bf16[768,1152]{1,0:T(8,128)(2,1)} %param.16) | copy-start | bytes 5308420
  7.2 129.4 %all-gather.7.cloned.1.call-start = ((), (), s32[]{:S(2)}) async-start(), calls=%async_computation.3 | async-start | bytes 1966080 | tf_op jit(solution)/shard_map/all_gather | solution.py:172
  7.9 131.9 %all-gather.9.cloned.1.call-start = ((), (), s32[]{:S(2)}) async-start(), calls=%async_computation.6 | async-start | bytes 2654208 | tf_op jit(solution)/shard_map/all_gather | solution.py:165
  8.7 118.4 %copy-start.6 = (bf16[1,48,3072]{2,1,0:T(8,128)(2,1)S(1)}, bf16[1,48,3072]{2,1,0:T(8,128)(2,1)}, u32[]{:S(2)}) copy-start(bf16[1,48,3072]{2,1,0:T(8,128)(2,1)} %param.19) | copy-start | bytes 884740
  8.7 135.7 %all-gather.5.cloned.1.call-start = ((), (), s32[]{:S(2)}) async-start(), calls=%async_computation.2 | async-start | bytes 5898240 | tf_op jit(solution)/shard_map/all_gather | solution.py:170
  8.7 13.3 %collective-permute-start = (bf16[48,3072]{1,0:T(8,128)(2,1)}, bf16[48,3072]{1,0:T(8,128)(2,1)S(1)}, u32[]{:S(2)}, u32[]{:S(2)}) collective-permute-start(bf16[48,3072]{1,0:T(8,128)(2,1)} %bitcast.159), channel_id=1, source_target_pairs={{0,1},{1,2},{2,3},{3,4},{4,5},{5,6},{6,7},{7,0},{8,9},{9,10},{10,1... | collective-permute-start | bytes 884744 | tf_op jit(solution)/shard_map/ppermute | solution.py:15
  11.8 251.7 %reduce-scatter.5.cloned.1.call-start = ((), (), s32[]{:S(2)}) async-start(), calls=%async_computation.5 | async-start | bytes 2654208 | tf_op jit(solution)/shard_map/reduce_scatter | solution.py:183
  22.0 10.9 %collective-permute-start.1 = (bf16[48,3072]{1,0:T(8,128)(2,1)S(1)}, bf16[48,3072]{1,0:T(8,128)(2,1)S(1)}, u32[]{:S(2)}, u32[]{:S(2)}) collective-permute-start(bf16[48,3072]{1,0:T(8,128)(2,1)S(1)} %collective-permute-done), channel_id=1, source_target_pairs={{0,1},{1,2},{2,3},{3,4},{4,5},{5,6},{6,7},{7,0},{8,9},{9,10},{10,1... | collective-permute-start | bytes 884744 | tf_op jit(solution)/shard_map/ppermute | solution.py:15
  32.9 39.3 %collective-permute-start.2 = (bf16[48,3072]{1,0:T(8,128)(2,1)S(1)}, bf16[48,3072]{1,0:T(8,128)(2,1)S(1)}, u32[]{:S(2)}, u32[]{:S(2)}) collective-permute-start(bf16[48,3072]{1,0:T(8,128)(2,1)S(1)} %collective-permute-done.1), channel_id=1, source_target_pairs={{0,1},{1,2},{2,3},{3,4},{4,5},{5,6},{6,7},{7,0},{8,9},{9,10},{10,1... | collective-permute-start | bytes 884744 | tf_op jit(solution)/shard_map/ppermute | solution.py:15
  72.2 14.4 %collective-permute-start.3 = (bf16[48,3072]{1,0:T(8,128)(2,1)S(1)}, bf16[48,3072]{1,0:T(8,128)(2,1)S(1)}, u32[]{:S(2)}, u32[]{:S(2)}) collective-permute-start(bf16[48,3072]{1,0:T(8,128)(2,1)S(1)} %collective-permute-done.2), channel_id=1, source_target_pairs={{0,1},{1,2},{2,3},{3,4},{4,5},{5,6},{6,7},{7,0},{8,9},{9,10},{10,1... | collective-permute-start | bytes 884744 | tf_op jit(solution)/shard_map/ppermute | solution.py:15
  86.6 11.7 %copy-start.7 = (bf16[48,3072]{1,0:T(8,128)(2,1)}, bf16[48,3072]{1,0:T(8,128)(2,1)S(1)}, u32[]{:S(2)}) copy-start(bf16[48,3072]{1,0:T(8,128)(2,1)S(1)} %collective-permute-done.3) | copy-start | bytes 884740
  86.6 11.6 %collective-permute-start.4 = (bf16[48,3072]{1,0:T(8,128)(2,1)S(1)}, bf16[48,3072]{1,0:T(8,128)(2,1)}, u32[]{:S(2)}, u32[]{:S(2)}) collective-permute-start(bf16[48,3072]{1,0:T(8,128)(2,1)S(1)} %collective-permute-done.3), channel_id=1, source_target_pairs={{0,1},{1,2},{2,3},{3,4},{4,5},{5,6},{6,7},{7,0},{8,9},{9,10},{10,1... | collective-permute-start | bytes 884744 | tf_op jit(solution)/shard_map/ppermute | solution.py:15
  98.2 10.1 %collective-permute-start.5 = (bf16[48,3072]{1,0:T(8,128)(2,1)}, bf16[48,3072]{1,0:T(8,128)(2,1)}, u32[]{:S(2)}, u32[]{:S(2)}) collective-permute-start(bf16[48,3072]{1,0:T(8,128)(2,1)} %collective-permute-done.4), channel_id=1, source_target_pairs={{0,1},{1,2},{2,3},{3,4},{4,5},{5,6},{6,7},{7,0},{8,9},{9,10},{10,1... | collective-permute-start | bytes 884744 | tf_op jit(solution)/shard_map/ppermute | solution.py:15
  108.3 9.7 %collective-permute-start.6 = (bf16[48,3072]{1,0:T(8,128)(2,1)}, bf16[48,3072]{1,0:T(8,128)(2,1)}, u32[]{:S(2)}, u32[]{:S(2)}) collective-permute-start(bf16[48,3072]{1,0:T(8,128)(2,1)} %collective-permute-done.5), channel_id=1, source_target_pairs={{0,1},{1,2},{2,3},{3,4},{4,5},{5,6},{6,7},{7,0},{8,9},{9,10},{10,1... | collective-permute-start | bytes 884744 | tf_op jit(solution)/shard_map/ppermute | solution.py:15
  108.9 23.9 %copy-start.8 = (bf16[48,3072]{1,0:T(8,128)(2,1)S(1)}, bf16[48,3072]{1,0:T(8,128)(2,1)}, u32[]{:S(2)}) copy-start(bf16[48,3072]{1,0:T(8,128)(2,1)} %copy-done.7) | copy-start | bytes 884740
  109.7 26.9 %copy-start.13 = (f32[1,3072]{1,0:T(1,128)S(1)}, f32[1,3072]{1,0:T(1,128)}, u32[]{:S(2)}) copy-start(f32[1,3072]{1,0:T(1,128)} %get-tuple-element.23) | copy-start | bytes 36868
  139.8 22.2 %copy-start.9 = (bf16[384,256]{0,1:T(8,128)(2,1)}, bf16[384,256]{0,1:T(8,128)(2,1)S(1)}, u32[]{:S(2)}) copy-start(bf16[384,256]{0,1:T(8,128)(2,1)S(1)} %fusion.22) | copy-start | bytes 589828
  149.7 6.7 %copy-start.15 = (f32[1,3072]{1,0:T(1,128)S(1)}, f32[1,3072]{1,0:T(1,128)}, u32[]{:S(2)}) copy-start(f32[1,3072]{1,0:T(1,128)} %get-tuple-element.24) | copy-start | bytes 36868
  161.8 8.5 %copy-start.16 = (f32[128]{0:T(128)S(1)}, f32[128]{0:T(128)}, u32[]{:S(2)}) copy-start(f32[128]{0:T(128)} %constant.92.clone) | copy-start | bytes 1540
  163.4 8.8 %copy-start.2 = (f32[2,384,128]{1,2,0:T(8,128)}, f32[2,384,128]{1,2,0:T(8,128)S(1)}, u32[]{:S(2)}) copy-start(f32[2,384,128]{1,2,0:T(8,128)S(1)} %get-tuple-element.12) | copy-start | bytes 1179652
  163.4 16.8 %copy-start.1 = (f32[2,384,128]{1,2,0:T(8,128)}, f32[2,384,128]{1,2,0:T(8,128)S(1)}, u32[]{:S(2)}) copy-start(f32[2,384,128]{1,2,0:T(8,128)S(1)} %get-tuple-element.11) | copy-start | bytes 1179652
  180.2 12.8 %slice-start = ((s8[4718592]{0:T(1024)(128)(4,1)}), s8[524288]{0:T(1024)(128)(4,1)S(1)}, s32[]{:S(2)}) async-start(s8[4718592]{0:T(1024)(128)(4,1)} %bitcast.154), calls=%async_computation.7 | async-start | bytes 1048576
  196.6 139.0 %copy-start.14 = (f32[1,3072]{1,0:T(1,128)S(1)}, f32[1,3072]{1,0:T(1,128)}, u32[]{:S(2)}) copy-start(f32[1,3072]{1,0:T(1,128)} %get-tuple-element.23) | copy-start | bytes 36868
  196.6 139.0 %reduce-scatter.3.cloned.1.call-start = ((), (), s32[]{:S(2)}) async-start(), calls=%async_computation.4 | async-start | bytes 2654208 | tf_op jit(solution)/shard_map/reduce_scatter | solution.py:177
  (7 other events, 24.5 us)
Sparse Core Ops, SparseCore 0:
  9.5 22.3 all-gather.6
  34.1 55.9 all-gather.8
  91.7 40.4 all-gather.4
  196.8 66.6 reduce-scatter.4
  266.8 68.7 reduce-scatter.2
